TPU v7x, 32 devices: a whole 2x2x4 slice. The times are simulated.
32 devices in a mesh: leaf: 4 (over x, core), front: 8 (over z, y), wave: 1.
Axes of the slice: x: 2, y: 2, z: 4, core: 2. Of those that a mesh axis runs over, the one named last changes fastest.
Arguments:
- sources: float32 [8192, 128], P(('wave', 'front')), may hold values from -48 to 48
- order: int32 [8192], P('front'), may hold values from 0 to 8191, as said below
- diagonal: float32 [8192], P(('wave', 'front')), may hold values from 0.1 to 2
- coupling: float32 [8192, 4096], P(('wave', 'front'), 'leaf'), may hold values from -0.0625 to 0.0625
- interior_inverse: float32 [64, 64, 64], P(('wave', 'leaf')), may hold values from -2 to 6, as said below
- interior_load: float32 [64, 64, 128], P(('wave', 'leaf')), may hold values from -6 to 6
Outputs:
- solution: float32 [8192, 128], P(('wave', 'front'))
- interior_solution: float32 [64, 64, 128], P(('wave', 'leaf'))
Inputs may be any that keep to these rules, and one draw needn't show every extreme that they name: `order`: each aligned block of 1024 entries is a permutation of that block's own indices. `interior_inverse`: each matrix is symmetric positive definite.
All inputs are finite; a program needn't handle non-finite values.
Results may differ from a plain program's by a relative error of at most 0.0003.
Values sent between devices are 32-bit elements; how exact they have to be, the bound alone decides.
No kernel may reach another device: no remote copies, remote signals or barrier semaphores. Data moves between devices by JAX's collectives and lax.ppermute only.
A program may use at most 64 MiB of HBM per device.

v0:
```python
import jax
import jax.numpy as jnp
from jax import lax
from jax.sharding import PartitionSpec as P

ITERS = 4
HIGHEST = lax.Precision.HIGHEST


def couple(coupling, field):
    partial_sums = jnp.einsum("sk,sn->kn", coupling, field, precision=HIGHEST)
    return lax.psum(partial_sums, "front")


def condense(interior_inverse, projected):
    shaped = projected.reshape(
        interior_inverse.shape[0], interior_inverse.shape[1], projected.shape[1]
    )
    return jnp.einsum("bij,bjn->bin", interior_inverse, shaped, precision=HIGHEST)


def cg_update(solution, residual, direction, image, norm_now, own):
    mine_dir = own(direction)
    mine_res = own(residual)
    mine_img = own(image)
    curvature, cross, square = lax.psum(
        (
            jnp.sum(mine_dir * mine_img, axis=0),
            jnp.sum(mine_res * mine_img, axis=0),
            jnp.sum(mine_img * mine_img, axis=0),
        ),
        ("leaf", "front"),
    )
    step_size = norm_now / curvature
    norm_next = norm_now - 2.0 * step_size * cross + step_size * step_size * square
    solution = solution + step_size * direction
    residual = residual - step_size * image
    direction = residual + norm_next / norm_now * direction
    return (solution, residual, direction, norm_next)


def per_device(sources, order, diagonal, coupling, interior_inverse, interior_load):
    rows_here = sources.shape[0]
    columns = sources.shape[1]
    positions = order - lax.axis_index("front") * rows_here
    loads = jnp.take(sources, positions, axis=0)
    share_rows = rows_here // lax.axis_size("leaf")
    first_row = lax.axis_index("leaf") * share_rows

    def own_rows(field):
        return lax.dynamic_slice_in_dim(field, first_row, share_rows, 0)

    start_share = own_rows(loads)
    start_total = lax.psum(jnp.sum(start_share * start_share, axis=0), ("leaf", "front"))
    solution = jnp.zeros_like(loads)
    residual = loads
    direction = loads
    norm_now = start_total
    for iteration in range(ITERS):
        coeffs = condense(interior_inverse, couple(coupling, direction)).reshape(-1, columns)
        spread_term = jnp.einsum("sk,kn->sn", coupling, coeffs, precision=HIGHEST)
        image = diagonal[:, None] * direction + lax.psum(spread_term, "leaf")
        solution, residual, direction, norm_now = cg_update(
            solution, residual, direction, image, norm_now, own_rows
        )
    projected = couple(coupling, solution).reshape(interior_load.shape)
    interior_solution = jnp.einsum(
        "bij,bjn->bin", interior_inverse, interior_load - projected, precision=HIGHEST
    )
    return (solution, interior_solution)


def solution(mesh):
    return jax.shard_map(
        per_device,
        mesh=mesh,
        in_specs=(
            P(("wave", "front"), None),
            P("front"),
            P(("wave", "front")),
            P(("wave", "front"), "leaf"),
            P(("wave", "leaf"), None, None),
            P(("wave", "leaf"), None, None),
        ),
        out_specs=(P(("wave", "front"), None), P(("wave", "leaf"), None, None)),
        check_vma=False,
    )
```

profile of v0, /device:TPU:0, one launch (start us, length us, event | category | flops | bytes accessed | tf_op | source)
XLA Modules:
  0.0 752.2 jit_solution(4193403296460094578)
XLA Ops:
  7.2 0.0 all-reduce.13.cloned.1.call-start
  7.2 0.7 fusion.3
  8.0 0.7 compare_and_fusion
  8.7 3.8 gather_fusion
  12.5 0.2 copy.15
  12.8 4.6 convolution_bitcast_fusion.9
  17.4 1.0 copy.16
  18.4 0.0 all-reduce.13.cloned.1.call-update
  18.4 0.0 all-reduce.15.cloned.1.call-start
  18.4 75.6 %all-reduce.13.cloned.1.call-done = f32[16,64,128]{2,1,0:T(8,128)} async-done(((f32[16,64,128]{2,1,0:T(8,128)}), f32[16,64,128]{2,1,0:T(8,128)}) %all-reduce.13.cloned.1.call-update) | async-done | bytes 524304 | tf_op jit(solution)/shard_map/psum | solution.py:12
  94.0 1.7 fusion.7
  95.7 7.5 %convolution_bitcast_fusion.8 = f32[1024,128]{0,1:T(8,128)} fusion(f32[1024,128]{1,0:T(8,128)S(1)} %bitcast.64, f32[1024,1024]{1,0:T(8,128)} %param.9), kind=kOutput, calls=%fused_computation.9 | convolution fusion | flops 1610612736 | bytes 5242880 | tf_op jit(solution)/shard_map/sk,kn->sn/dot_general | solution.py:61
  103.2 0.0 all-reduce.15.cloned.1.call-update
  103.2 0.0 all-reduce.17.cloned.1.call-start
  103.3 32.7 %all-reduce.15.cloned.1.call-done = f32[1024,128]{0,1:T(8,128)} async-done(((f32[1024,128]{0,1:T(8,128)}), f32[1024,128]{0,1:T(8,128)}) %all-reduce.15.cloned.1.call-update) | async-done | bytes 524304 | tf_op jit(solution)/shard_map/psum | solution.py:62
  136.0 1.1 multiply_add_fusion.6
  137.1 0.2 multiply_reduce_fusion.6
  137.3 39.5 %all-reduce.2 = (f32[128]{0:T(128)S(1)}, f32[128]{0:T(128)S(1)}, f32[128]{0:T(128)S(1)}) all-reduce(f32[128]{0:T(128)S(1)} %get-tuple-element.14, f32[128]{0:T(128)S(1)} %get-tuple-element.13, f32[128]{0:T(128)S(1)} %get-tuple-element.12), channel_id=1, replica_groups=mesh['leaf'=4,'front'=8,'wave'=1] {'leaf','front'}, use_global_device_ids=true, to_apply=%region_1.2 | all-reduce | flops 384 | bytes 3072 | tf_op jit(solution)/shard_map/psum | solution.py:54
  176.7 0.2 multiply_add_fusion.5
  176.9 4.6 convolution_bitcast_fusion.7
  181.5 1.0 copy.17
  182.5 0.0 all-reduce.17.cloned.1.call-update
  182.5 0.2 all-reduce.19.cloned.1.call-start
  182.8 73.2 %all-reduce.17.cloned.1.call-done = f32[16,64,128]{2,1,0:T(8,128)} async-done(((f32[16,64,128]{2,1,0:T(8,128)}), f32[16,64,128]{2,1,0:T(8,128)}) %all-reduce.17.cloned.1.call-update) | async-done | bytes 524304 | tf_op jit(solution)/shard_map/psum | solution.py:12
  255.9 1.7 fusion.8
  257.6 7.5 convolution_bitcast_fusion.6
  265.0 0.0 all-reduce.19.cloned.1.call-update
  265.1 0.0 all-reduce.21.cloned.1.call-start
  265.1 32.7 %all-reduce.19.cloned.1.call-done = f32[1024,128]{0,1:T(8,128)} async-done(((f32[1024,128]{0,1:T(8,128)}), f32[1024,128]{0,1:T(8,128)}) %all-reduce.19.cloned.1.call-update) | async-done | bytes 524304 | tf_op jit(solution)/shard_map/psum | solution.py:62
  297.8 1.1 multiply_add_fusion.4
  298.9 0.2 multiply_reduce_fusion.4
  299.1 39.5 %all-reduce.1 = (f32[128]{0:T(128)S(1)}, f32[128]{0:T(128)S(1)}, f32[128]{0:T(128)S(1)}) all-reduce(f32[128]{0:T(128)S(1)} %get-tuple-element.11, f32[128]{0:T(128)S(1)} %get-tuple-element.10, f32[128]{0:T(128)S(1)} %get-tuple-element.9), channel_id=1, replica_groups=mesh['leaf'=4,'front'=8,'wave'=1] {'leaf','front'}, use_global_device_ids=true, to_apply=%region_11.12 | all-reduce | flops 384 | bytes 3072 | tf_op jit(solution)/shard_map/psum | solution.py:26
  338.6 1.0 multiply_add_fusion.3
  339.5 4.6 convolution_bitcast_fusion.5
  344.1 1.0 copy.18
  345.1 0.0 all-reduce.21.cloned.1.call-update
  345.1 0.3 all-reduce.23.cloned.1.call-start
  345.4 73.1 %all-reduce.21.cloned.1.call-done = f32[16,64,128]{2,1,0:T(8,128)} async-done(((f32[16,64,128]{2,1,0:T(8,128)}), f32[16,64,128]{2,1,0:T(8,128)}) %all-reduce.21.cloned.1.call-update) | async-done | bytes 524304 | tf_op jit(solution)/shard_map/psum | solution.py:12
  418.5 1.7 fusion.9
  420.2 7.5 convolution_bitcast_fusion.4
  427.7 0.0 all-reduce.23.cloned.1.call-update
  427.7 0.0 all-reduce.25.cloned.1.call-start
  427.7 32.7 %all-reduce.23.cloned.1.call-done = f32[1024,128]{0,1:T(8,128)} async-done(((f32[1024,128]{0,1:T(8,128)}), f32[1024,128]{0,1:T(8,128)}) %all-reduce.23.cloned.1.call-update) | async-done | bytes 524304 | tf_op jit(solution)/shard_map/psum | solution.py:62
  460.4 1.1 multiply_add_fusion.2
  461.6 0.2 multiply_reduce_fusion.1
  461.7 39.5 %all-reduce = (f32[128]{0:T(128)S(1)}, f32[128]{0:T(128)S(1)}, f32[128]{0:T(128)S(1)}) all-reduce(f32[128]{0:T(128)S(1)} %get-tuple-element.7, f32[128]{0:T(128)S(1)} %get-tuple-element.8, f32[128]{0:T(128)S(1)} %get-tuple-element.6), channel_id=1, replica_groups=mesh['leaf'=4,'front'=8,'wave'=1] {'leaf','front'}, use_global_device_ids=true, to_apply=%region_23.24 | all-reduce | flops 384 | bytes 3072 | tf_op jit(solution)/shard_map/psum | solution.py:26
  501.2 1.2 multiply_add_fusion.1
  502.4 4.6 convolution_bitcast_fusion.3
  507.0 1.0 copy.19
  508.0 0.3 all-reduce.27.cloned.1.call-start
  508.4 73.1 %all-reduce.25.cloned.1.call-done = f32[16,64,128]{2,1,0:T(8,128)} async-done(((f32[16,64,128]{2,1,0:T(8,128)}), f32[16,64,128]{2,1,0:T(8,128)}) %all-reduce.25.cloned.1.call-update) | async-done | bytes 524304 | tf_op jit(solution)/shard_map/psum | solution.py:12
  581.4 1.7 fusion.10
  583.1 7.5 %convolution_bitcast_fusion.2 = f32[1024,128]{0,1:T(8,128)} fusion(f32[1024,128]{1,0:T(8,128)S(1)} %bitcast.67, f32[1024,1024]{1,0:T(8,128)} %param.9), kind=kOutput, calls=%fused_computation.3 | convolution fusion | flops 1610612736 | bytes 5242880 | tf_op jit(solution)/shard_map/sk,kn->sn/dot_general | solution.py:61
  590.7 0.0 all-reduce.29.cloned.1.call-start
  590.7 0.1 dynamic-slice
  590.8 32.6 %all-reduce.27.cloned.1.call-done = f32[1024,128]{0,1:T(8,128)} async-done(((f32[1024,128]{0,1:T(8,128)}), f32[1024,128]{0,1:T(8,128)}) %all-reduce.27.cloned.1.call-update) | async-done | bytes 524304 | tf_op jit(solution)/shard_map/psum | solution.py:62
  623.4 1.0 fusion.2
  624.4 39.4 %psum.153 = f32[128]{0:T(128)S(1)} all-reduce(f32[128]{0:T(128)S(1)} %fusion.2), channel_id=1, replica_groups=mesh['leaf'=4,'front'=8,'wave'=1] {'leaf','front'}, use_global_device_ids=true, to_apply=%region_27.28 | all-reduce | flops 128 | bytes 1024 | tf_op jit(solution)/shard_map/psum | solution.py:26
  663.9 0.2 multiply_add_fusion
  664.1 4.6 convolution_bitcast_fusion.1
  668.8 1.0 copy.20
  669.8 1.0 copy.21
  670.8 72.4 %all-reduce.29.cloned.1.call-done = f32[16,64,128]{2,1,0:T(8,128)} async-done(((f32[16,64,128]{2,1,0:T(8,128)}), f32[16,64,128]{2,1,0:T(8,128)}) %all-reduce.29.cloned.1.call-update) | async-done | bytes 524304 | tf_op jit(solution)/shard_map/psum | solution.py:12
  743.2 2.5 convolution_bitcast_fusion
  (16 shorter events, 0.1 us)
Async XLA Ops:
  7.2 86.8 %copy-start = (f32[16,64,64]{2,1,0:T(8,128)S(1)}, f32[16,64,64]{2,1,0:T(8,128)}, u32[]{:S(2)}) copy-start(f32[16,64,64]{2,1,0:T(8,128)} %param.10) | copy-start | bytes 786436
  7.2 86.8 %all-reduce.13.cloned.1.call-start = ((), (), s32[]{:S(2)}) async-start(), calls=%async_computation | async-start | bytes 1048576 | tf_op jit(solution)/shard_map/psum | solution.py:12
  18.4 117.6 %copy-start.3 = (f32[1024]{0:T(1024)S(1)}, f32[1024]{0:T(1024)}, u32[]{:S(2)}) copy-start(f32[1024]{0:T(1024)} %param.8) | copy-start | bytes 12292
  18.4 117.6 %all-reduce.15.cloned.1.call-start = ((), (), s32[]{:S(2)}) async-start(), calls=%async_computation.1 | async-start | bytes 1048576 | tf_op jit(solution)/shard_map/psum | solution.py:62
  103.2 152.7 %all-reduce.17.cloned.1.call-start = ((), (), s32[]{:S(2)}) async-start(), calls=%async_computation.2 | async-start | bytes 1048576 | tf_op jit(solution)/shard_map/psum | solution.py:12
  182.5 115.3 %all-reduce.19.cloned.1.call-start = ((), (), s32[]{:S(2)}) async-start(), calls=%async_computation.3 | async-start | bytes 1048576 | tf_op jit(solution)/shard_map/psum | solution.py:62
  265.1 153.5 %all-reduce.21.cloned.1.call-start = ((), (), s32[]{:S(2)}) async-start(), calls=%async_computation.4 | async-start | bytes 1048576 | tf_op jit(solution)/shard_map/psum | solution.py:12
  345.1 116.4 %copy-start.1 = (f32[1024,128]{0,1:T(8,128)S(1)}, f32[1024,128]{0,1:T(8,128)}, u32[]{:S(2)}) copy-start(f32[1024,128]{0,1:T(8,128)} %get-tuple-element.28) | copy-start | bytes 1572868
  345.1 115.3 %all-reduce.23.cloned.1.call-start = ((), (), s32[]{:S(2)}) async-start(), calls=%async_computation.5 | async-start | bytes 1048576 | tf_op jit(solution)/shard_map/psum | solution.py:62
  427.7 153.7 %all-reduce.25.cloned.1.call-start = ((), (), s32[]{:S(2)}) async-start(), calls=%async_computation.6 | async-start | bytes 1048576 | tf_op jit(solution)/shard_map/psum | solution.py:12
  508.0 115.4 %all-reduce.27.cloned.1.call-start = ((), (), s32[]{:S(2)}) async-start(), calls=%async_computation.7 | async-start | bytes 1048576 | tf_op jit(solution)/shard_map/psum | solution.py:62
  590.7 152.5 %all-reduce.29.cloned.1.call-start = ((), (), s32[]{:S(2)}) async-start(), calls=%async_computation.8 | async-start | bytes 1048576 | tf_op jit(solution)/shard_map/psum | solution.py:12
  664.1 79.1 %copy-start.2 = (f32[16,64,128]{2,1,0:T(8,128)S(1)}, f32[16,64,128]{2,1,0:T(8,128)}, u32[]{:S(2)}) copy-start(f32[16,64,128]{2,1,0:T(8,128)} %param.11) | copy-start | bytes 1572868
Sparse Core Ops, SparseCore 0:
  18.5 75.4 all-reduce.12
  103.3 32.5 all-reduce.14
  182.6 73.2 all-reduce.16
  265.2 32.5 all-reduce.18
  345.3 73.2 all-reduce.20
  427.8 32.5 all-reduce.22
  508.2 73.2 all-reduce.24
  590.8 32.5 all-reduce.26
  669.9 73.2 all-reduce.28
where the time goes:
time: 753 us; the launch traced here: 752 us
  waiting for transfers between devices  498 us (66%)
  blocking collectives  158 us (21%)
  matrix products  62.1 us (8%)
  between operations  14 us (2%)
  local copies, waits for them, and re-layouts  10.1 us (1%)
  other arithmetic  8.92 us (1%)
    psum x5, waiting for transfers between devices, couple(): return lax.psum(partial_sums, 'front')  367 us
    psum x4, waiting for transfers between devices, per_device(): image = diagonal[:, None] * direction + lax.psum(spread_term, 'leaf')  131 us
    psum x3, blocking collectives, cg_update(): lax.psum((jnp.sum(mine_dir * mine_img, axis=0), jnp.sum(mine_res * mine_i...  118 us
    psum x1, blocking collectives, per_device(): lax.psum(jnp.sum(start_share * start_share, axis=0), ('leaf', 'front'))  39.5 us
    dot_general x4, matrix products, per_device(): spread_term = jnp.einsum('sk,kn->sn', coupling, coeffs, precision=HIGHEST)  30 us
    dot_general x5, matrix products, couple(): partial_sums = jnp.einsum('sk,sn->kn', coupling, field, precision=HIGHEST)  23 us
  transfers between devices with their start and end apart: 9, of which 9 were waited for; matrix products, arithmetic and copies ran while one was open for 0% of the time, Pallas kernels for 0%

commit v1 on v0

--- a/solution.py
+++ b/solution.py
@@ -5,6 +5,10 @@
 
 ITERS = 4
 HIGHEST = lax.Precision.HIGHEST
+
+
+def ratios_step_on(buf):
+    return lax.all_gather(buf, "leaf").sum(axis=0)
 
 
 def couple(coupling, field):
@@ -59,7 +63,7 @@
     for iteration in range(ITERS):
         coeffs = condense(interior_inverse, couple(coupling, direction)).reshape(-1, columns)
         spread_term = jnp.einsum("sk,kn->sn", coupling, coeffs, precision=HIGHEST)
-        image = diagonal[:, None] * direction + lax.psum(spread_term, "leaf")
+        image = diagonal[:, None] * direction + ratios_step_on(spread_term)
         solution, residual, direction, norm_now = cg_update(
             solution, residual, direction, image, norm_now, own_rows
         )

time: 753 us -> 744 us (0.988); the launches traced: 752 us -> 736 us
  waiting for transfers between devices: 498 us -> 457 us
  local copies, waits for them, and re-layouts: 10.1 us -> 25 us
  other arithmetic: 8.92 us -> 17.9 us
    psum x4 -> x0, waiting for transfers between devices: 131 us -> none  [per_device(): image = diagonal[:, None] * direction + lax.psum(spread_term, 'leaf')]
    all_gather x0 -> x4, waiting for transfers between devices: none -> 87.3 us  [ratios_step_on(): return lax.all_gather(buf, 'leaf').sum(axis=0)]
    all_gather x0 -> x4, local copies, waits for them, and re-layouts: none -> 13.6 us  [ratios_step_on(): return lax.all_gather(buf, 'leaf').sum(axis=0)]
    reduce_sum x0 -> x4, other arithmetic: none -> 10.8 us  [ratios_step_on(): return lax.all_gather(buf, 'leaf').sum(axis=0)]
where the time goes in v1:
time: 744 us; the launch traced here: 736 us
  waiting for transfers between devices  457 us (61%)
  blocking collectives  159 us (21%)
  matrix products  62.4 us (8%)
  local copies, waits for them, and re-layouts  25 us (3%)
  other arithmetic  17.9 us (2%)
  between operations  14.4 us (2%)
    psum x5, waiting for transfers between devices, couple(): return lax.psum(partial_sums, 'front')  370 us
    psum x3, blocking collectives, cg_update(): lax.psum((jnp.sum(mine_dir * mine_img, axis=0), jnp.sum(mine_res * mine_i...  119 us
    all_gather x4, waiting for transfers between devices, ratios_step_on(): return lax.all_gather(buf, 'leaf').sum(axis=0)  87.3 us
    psum x1, blocking collectives, per_device(): lax.psum(jnp.sum(start_share * start_share, axis=0), ('leaf', 'front'))  39.9 us
    dot_general x4, matrix products, per_device(): spread_term = jnp.einsum('sk,kn->sn', coupling, coeffs, precision=HIGHEST)  30.1 us
    dot_general x5, matrix products, couple(): partial_sums = jnp.einsum('sk,sn->kn', coupling, field, precision=HIGHEST)  23.2 us
  transfers between devices with their start and end apart: 9, of which 9 were waited for; matrix products, arithmetic and copies ran while one was open for 0% of the time, Pallas kernels for 0%

profile of v1, /device:TPU:0, one launch (start us, length us, event | category | flops | bytes accessed | tf_op | source)
XLA Modules:
  0.0 735.6 jit_solution(1935537549307374871)
XLA Ops:
  7.2 0.7 fusion.1
  8.0 0.7 compare_and_fusion
  8.7 3.8 gather_fusion
  12.5 0.2 broadcast_select_fusion
  12.7 0.8 copy-done.1
  13.5 4.7 convolution_bitcast_fusion.9
  18.2 1.0 copy.18
  19.2 0.0 all-gather.9.cloned.1.call-start
  19.3 75.6 %all-reduce.9.cloned.1.call-done = f32[16,64,128]{2,1,0:T(8,128)} async-done(((f32[16,64,128]{2,1,0:T(8,128)}), f32[16,64,128]{2,1,0:T(8,128)}) %all-reduce.9.cloned.1.call-update) | async-done | bytes 524304 | tf_op jit(solution)/shard_map/psum | solution.py:16
  94.8 1.7 fusion.5
  96.5 7.6 %convolution_bitcast_fusion.8 = f32[1024,128]{0,1:T(8,128)} fusion(f32[1024,128]{1,0:T(8,128)S(1)} %bitcast.72, f32[1024,1024]{1,0:T(8,128)} %param.9), kind=kOutput, calls=%fused_computation.9 | convolution fusion | flops 1610612736 | bytes 5242880 | tf_op jit(solution)/shard_map/sk,kn->sn/dot_general | solution.py:65
  104.1 0.0 all-reduce.11.cloned.1.call-start
  104.1 21.8 %all-gather.9.cloned.1.call-done = f32[4096,128]{0,1:T(8,128)} async-done(((f32[1024,128]{0,1:T(8,128)}), f32[4096,128]{0,1:T(8,128)}) %all-gather.9.cloned.1.call-update) | async-done | bytes 2097168 | tf_op jit(solution)/shard_map/all_gather | solution.py:11
  126.0 2.7 reshape.61
  128.7 2.2 reduce_sum.131
  130.9 1.2 copy.19
  132.1 0.3 multiply_add_fusion.6
  132.4 1.0 multiply_reduce_fusion.7
  133.4 39.9 %all-reduce.2 = (f32[128]{0:T(128)S(1)}, f32[128]{0:T(128)S(1)}, f32[128]{0:T(128)S(1)}) all-reduce(f32[128]{0:T(128)S(1)} %get-tuple-element.10, f32[128]{0:T(128)S(1)} %get-tuple-element.9, f32[128]{0:T(128)S(1)} %get-tuple-element.8), channel_id=1, replica_groups=mesh['leaf'=4,'front'=8,'wave'=1] {'leaf','front'}, use_global_device_ids=true, to_apply=%region_1.2 | all-reduce | flops 384 | bytes 3072 | tf_op jit(solution)/shard_map/psum | solution.py:58
  173.3 0.2 multiply_add_fusion.5
  173.5 4.6 convolution_bitcast_fusion.7
  178.1 1.0 copy.20
  179.1 0.0 all-gather.11.cloned.1.call-start
  179.2 73.5 %all-reduce.11.cloned.1.call-done = f32[16,64,128]{2,1,0:T(8,128)} async-done(((f32[16,64,128]{2,1,0:T(8,128)}), f32[16,64,128]{2,1,0:T(8,128)}) %all-reduce.11.cloned.1.call-update) | async-done | bytes 524304 | tf_op jit(solution)/shard_map/psum | solution.py:16
  252.7 1.7 fusion.6
  254.3 7.5 %convolution_bitcast_fusion.6 = f32[1024,128]{0,1:T(8,128)} fusion(f32[1024,128]{1,0:T(8,128)S(1)} %bitcast.73, f32[1024,1024]{1,0:T(8,128)} %param.9), kind=kOutput, calls=%fused_computation.7 | convolution fusion | flops 1610612736 | bytes 5242880 | tf_op jit(solution)/shard_map/sk,kn->sn/dot_general | solution.py:65
  261.9 21.8 %all-gather.11.cloned.1.call-done = f32[4096,128]{0,1:T(8,128)} async-done(((f32[1024,128]{0,1:T(8,128)}), f32[4096,128]{0,1:T(8,128)}) %all-gather.11.cloned.1.call-update) | async-done | bytes 2097168 | tf_op jit(solution)/shard_map/all_gather | solution.py:11
  283.7 3.6 reshape.62
  287.3 2.9 reduce_sum.134
  290.2 0.2 copy.21
  290.4 0.2 multiply_add_fusion.4
  290.6 0.1 multiply_reduce_fusion.5
  290.7 39.5 %all-reduce.1 = (f32[128]{0:T(128)S(1)}, f32[128]{0:T(128)S(1)}, f32[128]{0:T(128)S(1)}) all-reduce(f32[128]{0:T(128)S(1)} %get-tuple-element.7, f32[128]{0:T(128)S(1)} %get-tuple-element.6, f32[128]{0:T(128)S(1)} %get-tuple-element.5), channel_id=1, replica_groups=mesh['leaf'=4,'front'=8,'wave'=1] {'leaf','front'}, use_global_device_ids=true, to_apply=%region_11.12 | all-reduce | flops 384 | bytes 3072 | tf_op jit(solution)/shard_map/psum | solution.py:30
  330.2 0.9 multiply_add_fusion.3
  331.1 4.6 convolution_bitcast_fusion.5
  335.7 1.0 copy.22
  336.8 73.5 %all-reduce.13.cloned.1.call-done = f32[16,64,128]{2,1,0:T(8,128)} async-done(((f32[16,64,128]{2,1,0:T(8,128)}), f32[16,64,128]{2,1,0:T(8,128)}) %all-reduce.13.cloned.1.call-update) | async-done | bytes 524304 | tf_op jit(solution)/shard_map/psum | solution.py:16
  410.3 1.7 fusion.7
  411.9 7.5 %convolution_bitcast_fusion.4 = f32[1024,128]{0,1:T(8,128)} fusion(f32[1024,128]{1,0:T(8,128)S(1)} %bitcast.74, f32[1024,1024]{1,0:T(8,128)} %param.9), kind=kOutput, calls=%fused_computation.5 | convolution fusion | flops 1610612736 | bytes 5242880 | tf_op jit(solution)/shard_map/sk,kn->sn/dot_general | solution.py:65
  419.5 21.8 %all-gather.13.cloned.1.call-done = f32[4096,128]{0,1:T(8,128)} async-done(((f32[1024,128]{0,1:T(8,128)}), f32[4096,128]{0,1:T(8,128)}) %all-gather.13.cloned.1.call-update) | async-done | bytes 2097168 | tf_op jit(solution)/shard_map/all_gather | solution.py:11
  441.4 3.6 reshape.63
  445.0 2.9 reduce_sum.138
  447.9 0.2 copy.23
  448.1 0.2 multiply_add_fusion.2
  448.3 1.0 multiply_reduce_fusion.2
  449.3 39.6 %all-reduce = (f32[128]{0:T(128)S(1)}, f32[128]{0:T(128)S(1)}, f32[128]{0:T(128)S(1)}) all-reduce(f32[128]{0:T(128)S(1)} %get-tuple-element.3, f32[128]{0:T(128)S(1)} %get-tuple-element.4, f32[128]{0:T(128)S(1)} %get-tuple-element.2), channel_id=1, replica_groups=mesh['leaf'=4,'front'=8,'wave'=1] {'leaf','front'}, use_global_device_ids=true, to_apply=%region_23.24 | all-reduce | flops 384 | bytes 3072 | tf_op jit(solution)/shard_map/psum | solution.py:30
  488.8 1.2 multiply_add_fusion.1
  490.1 4.6 convolution_bitcast_fusion.3
  494.7 1.0 copy.24
  495.7 73.5 %all-reduce.15.cloned.1.call-done = f32[16,64,128]{2,1,0:T(8,128)} async-done(((f32[16,64,128]{2,1,0:T(8,128)}), f32[16,64,128]{2,1,0:T(8,128)}) %all-reduce.15.cloned.1.call-update) | async-done | bytes 524304 | tf_op jit(solution)/shard_map/psum | solution.py:16
  569.2 1.7 fusion.8
  570.9 7.5 %convolution_bitcast_fusion.2 = f32[1024,128]{0,1:T(8,128)} fusion(f32[1024,128]{1,0:T(8,128)S(1)} %bitcast.75, f32[1024,1024]{1,0:T(8,128)} %param.9), kind=kOutput, calls=%fused_computation.3 | convolution fusion | flops 1610612736 | bytes 5242880 | tf_op jit(solution)/shard_map/sk,kn->sn/dot_general | solution.py:65
  578.5 0.1 dynamic-slice
  578.6 21.8 %all-gather.15.cloned.1.call-done = f32[4096,128]{0,1:T(8,128)} async-done(((f32[1024,128]{0,1:T(8,128)}), f32[4096,128]{0,1:T(8,128)}) %all-gather.15.cloned.1.call-update) | async-done | bytes 2097168 | tf_op jit(solution)/shard_map/all_gather | solution.py:11
  600.4 3.6 reshape.64
  604.0 2.9 reduce_sum.142
  606.9 0.1 copy.27
  607.0 0.1 multiply_reduce_fusion
  607.1 39.6 %psum.121 = f32[128]{0:T(128)S(1)} all-reduce(f32[128]{0:T(128)S(1)} %multiply_reduce_fusion), channel_id=1, replica_groups=mesh['leaf'=4,'front'=8,'wave'=1] {'leaf','front'}, use_global_device_ids=true, to_apply=%region_27.28 | all-reduce | flops 128 | bytes 1024 | tf_op jit(solution)/shard_map/psum | solution.py:30
  646.7 0.2 multiply_add_fusion
  646.9 4.8 convolution_bitcast_fusion.1
  651.7 1.0 copy.26
  652.8 73.6 %all-reduce.17.cloned.1.call-done = f32[16,64,128]{2,1,0:T(8,128)} async-done(((f32[16,64,128]{2,1,0:T(8,128)}), f32[16,64,128]{2,1,0:T(8,128)}) %all-reduce.17.cloned.1.call-update) | async-done | bytes 524304 | tf_op jit(solution)/shard_map/psum | solution.py:16
  726.3 2.5 convolution_bitcast_fusion
  (29 shorter events, 0.5 us)
Async XLA Ops:
  7.2 87.7 %copy-start = (f32[16,64,64]{2,1,0:T(8,128)S(1)}, f32[16,64,64]{2,1,0:T(8,128)}, u32[]{:S(2)}) copy-start(f32[16,64,64]{2,1,0:T(8,128)} %param.10) | copy-start | bytes 786436
  7.2 87.7 %all-reduce.9.cloned.1.call-start = ((), (), s32[]{:S(2)}) async-start(), calls=%async_computation | async-start | bytes 1048576 | tf_op jit(solution)/shard_map/psum | solution.py:16
  12.7 0.8 copy-start.1
  19.2 106.7 %all-gather.9.cloned.1.call-start = ((), (), s32[]{:S(2)}) async-start(), calls=%async_computation.5 | async-start | bytes 2621440 | tf_op jit(solution)/shard_map/all_gather | solution.py:11
  104.1 28.0 %copy-start.4 = (f32[1024]{0:T(1024)S(1)}, f32[1024]{0:T(1024)}, u32[]{:S(2)}) copy-start(f32[1024]{0:T(1024)} %param.8) | copy-start | bytes 12292
  104.1 148.6 %all-reduce.11.cloned.1.call-start = ((), (), s32[]{:S(2)}) async-start(), calls=%async_computation.1 | async-start | bytes 1048576 | tf_op jit(solution)/shard_map/psum | solution.py:16
  179.1 104.6 %all-gather.11.cloned.1.call-start = ((), (), s32[]{:S(2)}) async-start(), calls=%async_computation.6 | async-start | bytes 2621440 | tf_op jit(solution)/shard_map/all_gather | solution.py:11
  261.8 148.4 %all-reduce.13.cloned.1.call-start = ((), (), s32[]{:S(2)}) async-start(), calls=%async_computation.2 | async-start | bytes 1048576 | tf_op jit(solution)/shard_map/psum | solution.py:16
  336.7 104.7 %all-gather.13.cloned.1.call-start = ((), (), s32[]{:S(2)}) async-start(), calls=%async_computation.7 | async-start | bytes 2621440 | tf_op jit(solution)/shard_map/all_gather | solution.py:11
  419.5 149.8 %all-reduce.15.cloned.1.call-start = ((), (), s32[]{:S(2)}) async-start(), calls=%async_computation.3 | async-start | bytes 1048576 | tf_op jit(solution)/shard_map/psum | solution.py:16
  495.7 104.7 %all-gather.15.cloned.1.call-start = ((), (), s32[]{:S(2)}) async-start(), calls=%async_computation.8 | async-start | bytes 2621440 | tf_op jit(solution)/shard_map/all_gather | solution.py:11
  578.5 147.9 %all-reduce.17.cloned.1.call-start = ((), (), s32[]{:S(2)}) async-start(), calls=%async_computation.4 | async-start | bytes 1048576 | tf_op jit(solution)/shard_map/psum | solution.py:16
  646.9 81.9 %copy-start.2 = (f32[1024,128]{1,0:T(8,128)}, f32[1024,128]{1,0:T(8,128)S(1)}, u32[]{:S(2)}) copy-start(f32[1024,128]{1,0:T(8,128)S(1)} %multiply_add_fusion) | copy-start | bytes 1572868
  646.9 79.4 %copy-start.3 = (f32[16,64,128]{2,1,0:T(8,128)S(1)}, f32[16,64,128]{2,1,0:T(8,128)}, u32[]{:S(2)}) copy-start(f32[16,64,128]{2,1,0:T(8,128)} %param.11) | copy-start | bytes 1572868
Sparse Core Ops, SparseCore 0:
  19.4 75.4 all-reduce.8
  104.2 21.7 all-gather.8
  179.2 73.3 all-reduce.10
  261.9 21.7 all-gather.10
  336.8 73.3 all-reduce.12
  419.6 21.7 all-gather.12
  495.8 73.3 all-reduce.14
  578.6 21.7 all-gather.14
  652.9 73.4 all-reduce.16
